TPU v7x, 32 devices: a whole 2x2x4 slice. The times are simulated.
32 devices in a mesh: gz: 8 (over z, core), grp: 4 (over y, x).
Axes of the slice: x: 2, y: 2, z: 4, core: 2. Of those that a mesh axis runs over, the one named last changes fastest.
Arguments:
- volumes: bfloat16 [4, 16, 16, 1024], P('grp', 'gz'), may hold values from -6 to 6
- cotangent: bfloat16 [4, 8, 64, 128], P(None, 'gz', None, 'grp'), may hold values from -6 to 6
- fine_kernel: bfloat16 [1728, 64], replicated, may hold values from -0.15625 to 0.15625
- down_kernel: bfloat16 [512, 128], replicated, may hold values from -0.25 to 0.25
- coarse_kernel: bfloat16 [3456, 128], P(None, 'grp'), may hold values from -0.109375 to 0.109375
Outputs:
- coarse_out: bfloat16 [4, 8, 64, 128], P(None, 'gz', None, 'grp')
- volume_grad: bfloat16 [4, 16, 16, 1024], P('grp', 'gz')
- fine_kernel_grad: float32 [1728, 64], replicated
- down_kernel_grad: float32 [512, 128], replicated
- coarse_kernel_grad: float32 [3456, 128], P(None, 'grp')
All inputs are finite; a program needn't handle non-finite values.
Results may differ from a plain program's by a relative error of at most 0.019.
Values may be sent and summed in bfloat16 or wider, within the bound.
A program may use at most 64 MiB of HBM per device.

v0:
```python
import jax
import jax.numpy as jnp
from jax import lax
from jax.sharding import PartitionSpec as P


def with_halo(array, sides, width):
    for axis, dim in sides:
        devices, length = (lax.axis_size(axis), array.shape[dim])
        up = [(i, (i + 1) % devices) for i in range(devices - 1)]
        down = [(j, i) for i, j in up]
        last = lax.slice_in_dim(array, length - width, length, axis=dim)
        initial = lax.slice_in_dim(array, 0, width, axis=dim)
        before = lax.ppermute(last, axis, up)
        after = lax.ppermute(initial, axis, down)
        array = jnp.concatenate([before, array, after], axis=dim)
    return array


def pad_sides(block):
    return jnp.pad(block, ((0, 0), (0, 0), (1, 1), (1, 1), (0, 0)))


def convolve(padded, kernel):
    samples, extent_z, extent_x, extent_y, channels = padded.shape
    extent_z, extent_x, extent_y = (extent_z - 2, extent_x - 2, extent_y - 2)
    summed = None
    for plane in range(3):
        pieces = [
            padded[
                :,
                plane : plane + extent_z,
                row_step : row_step + extent_x,
                col_step : col_step + extent_y,
                :,
            ]
            for row_step in range(3)
            for col_step in range(3)
        ]
        columns = jnp.concatenate(pieces, axis=-1).reshape(-1, 9 * channels)
        rows = kernel[plane * 9 * channels : (plane + 1) * 9 * channels]
        partial_value = jnp.dot(columns, rows, preferred_element_type=jnp.float32)
        summed = partial_value if summed is None else summed + partial_value
    return summed.reshape(samples, extent_z, extent_x, extent_y, -1)


def kernel_gradient(padded, grad):
    samples, extent_z, extent_x, extent_y, channels = padded.shape
    extent_z, extent_x, extent_y = (extent_z - 2, extent_x - 2, extent_y - 2)
    flat_grad = grad.reshape(-1, grad.shape[-1])
    blocks = []
    for plane in range(3):
        pieces = [
            padded[
                :,
                plane : plane + extent_z,
                row_step : row_step + extent_x,
                col_step : col_step + extent_y,
                :,
            ]
            for row_step in range(3)
            for col_step in range(3)
        ]
        columns = jnp.concatenate(pieces, axis=-1).reshape(-1, 9 * channels)
        blocks.append(
            lax.dot_general(
                columns, flat_grad, (((0,), (0,)), ((), ())), preferred_element_type=jnp.float32
            )
        )
    return jnp.concatenate(blocks, axis=0)


def flip_kernel(kernel, inputs):
    outputs = kernel.shape[1]
    shaped = kernel.reshape(3, 3, 3, inputs, outputs)[::-1, ::-1, ::-1]
    return jnp.transpose(shaped, (0, 1, 2, 4, 3)).reshape(27 * outputs, inputs)


def silu_slope(value):
    sigmoid_v = jax.nn.sigmoid(value)
    return sigmoid_v * (1.0 + value * (1.0 - sigmoid_v))


def pool_columns(block):
    samples, extent_z, extent_x, extent_y, channels = block.shape
    shaped = block.reshape(samples, extent_z // 2, 2, extent_x // 2, 2, extent_y // 2, 2, channels)
    return jnp.transpose(shaped, (0, 1, 3, 5, 2, 4, 6, 7)).reshape(-1, 8 * channels)


def unpool_columns(flat, samples, extent_z, extent_x, extent_y, channels):
    shaped = flat.reshape(samples, extent_z // 2, extent_x // 2, extent_y // 2, 2, 2, 2, channels)
    return jnp.transpose(shaped, (0, 1, 4, 2, 5, 3, 6, 7)).reshape(
        samples, extent_z, extent_x, extent_y, channels
    )


def coarse_rim(block):
    return with_halo(block, (("gz", 1),), 1)


def coarse_grad_rim(block):
    return with_halo(block, (("gz", 1),), 1)


def coarse_kernel_total(partial_value):
    return lax.psum(partial_value.astype(jnp.bfloat16), "gz").astype(jnp.float32)


def per_device(volumes, cotangent, fine_kernel, down_kernel, coarse_kernel):
    samples, planes, xfine, packed = volumes.shape
    cfine = fine_kernel.shape[1]
    yfine = packed // cfine
    fine = volumes.reshape(samples, planes, xfine, yfine, cfine)
    fine_padded = pad_sides(with_halo(fine, (("gz", 1),), 1))
    fine_pre = convolve(fine_padded, fine_kernel)
    fine_act = jax.nn.silu(fine_pre).astype(jnp.bfloat16)
    pooled = pool_columns(fine_act)
    coarse_in = jnp.dot(pooled, down_kernel, preferred_element_type=jnp.float32).astype(
        jnp.bfloat16
    )
    coarse_in = coarse_in.reshape(samples, planes // 2, xfine // 2, yfine // 2, -1)
    coarse_framed = coarse_rim(coarse_in)
    gathered = pad_sides(lax.all_gather(coarse_framed, "grp", axis=0, tiled=True))
    coarse_pre = convolve(gathered, coarse_kernel)
    group, zcoarse, xcoarse, ycoarse, own_channels = coarse_pre.shape
    coarse_out = (
        jax.nn.silu(coarse_pre)
        .astype(jnp.bfloat16)
        .reshape(group, zcoarse, xcoarse * ycoarse, own_channels)
    )
    grad_shaped = cotangent.reshape(coarse_pre.shape).astype(jnp.float32)
    coarse_grad = (grad_shaped * silu_slope(coarse_pre)).astype(jnp.bfloat16)
    coarse_kg = coarse_kernel_total(kernel_gradient(gathered, coarse_grad))
    partial_value = convolve(
        pad_sides(coarse_grad_rim(coarse_grad)),
        flip_kernel(coarse_kernel, coarse_kernel.shape[0] // 27),
    )
    coarse_in_grad = lax.psum_scatter(
        partial_value.astype(jnp.bfloat16), "grp", scatter_dimension=0, tiled=True
    )
    flat_in_grad = coarse_in_grad.reshape(-1, coarse_in_grad.shape[-1])
    pooled_grad = jnp.dot(flat_in_grad, down_kernel.T, preferred_element_type=jnp.float32)
    fine_act_grad = unpool_columns(pooled_grad, samples, planes, xfine, yfine, cfine)
    down_kg = lax.dot_general(
        pooled, flat_in_grad, (((0,), (0,)), ((), ())), preferred_element_type=jnp.float32
    )
    fine_grad = (fine_act_grad * silu_slope(fine_pre)).astype(jnp.bfloat16)
    fine_kg = kernel_gradient(fine_padded, fine_grad)
    fine_kg, down_kg = lax.psum((fine_kg, down_kg), ("gz", "grp"))
    grad_padded = pad_sides(with_halo(fine_grad, (("gz", 1),), 1))
    volume_grad = convolve(grad_padded, flip_kernel(fine_kernel, cfine)).astype(jnp.bfloat16)
    volume_grad = volume_grad.reshape(samples, planes, xfine, packed)
    return (coarse_out, volume_grad, fine_kg, down_kg, coarse_kg)


def solution(mesh):
    in_specs = (P("grp", "gz", None, None), P(None, "gz", None, "grp"), P(), P(), P(None, "grp"))
    out_specs = (P(None, "gz", None, "grp"), P("grp", "gz", None, None), P(), P(), P(None, "grp"))
    return jax.shard_map(
        per_device, mesh=mesh, in_specs=in_specs, out_specs=out_specs, check_vma=False
    )
```

profile of v0, /device:TPU:0, one launch (start us, length us, event | category | flops | bytes accessed | tf_op | source)
XLA Modules:
  0.0 269.8 jit_solution(286053441385954328)
XLA Ops:
  8.1 1.1 reshape.446
  9.2 2.5 collective-permute-start
  11.7 1.3 collective-permute-start.1
  13.9 3.1 %collective-permute-done.1 = bf16[1,1,16,16,64]{4,3,2,1,0:T(8,128)(2,1)S(1)} collective-permute-done((bf16[1,1,16,16,64]{4,3,2,1,0:T(8,128)(2,1)S(1)}, bf16[1,1,16,16,64]{4,3,2,1,0:T(8,128)(2,1)S(1)}, u32[]{:S(2)}, u32[]{:S(2)}) %collective-permute-start.1) | collective-permute-done | bytes 32800 | tf_op jit(solution)/shard_map/ppermute | solution.py:15
  17.2 1.2 fusion.44
  19.7 1.0 fusion.26
  20.8 0.8 copy-done.36
  22.3 1.3 convolution_add_fusion.3
  26.6 4.8 %collective-permute-start.2 = (bf16[1,1,8,8,128]{4,3,2,0,1:T(8,128)(2,1)S(1)}, bf16[1,1,8,8,128]{4,3,2,0,1:T(8,128)(2,1)S(1)}, u32[]{:S(2)}, u32[]{:S(2)}) collective-permute-start(bf16[1,1,8,8,128]{4,3,2,0,1:T(8,128)(2,1)S(1)} %fusion.6), channel_id=1, source_target_pairs={{0,4},{4,8},{8,12},{12,16},{16,20},{20,24},{24,28},{1,5},{5,9},{9,... | collective-permute-start | bytes 49160 | tf_op jit(solution)/shard_map/ppermute | solution.py:14
  31.5 1.3 collective-permute-start.3
  33.5 0.7 copy.163
  37.3 2.9 %rev.7 = bf16[3,3,3,64,64]{3,2,1,0,4:T(4,128)(2,1)} reverse(bf16[3,3,3,64,64]{3,2,1,0,4:T(4,128)(2,1)S(1)} %reshape.464), dimensions={0,1,2} | reverse | bytes 442368 | tf_op jit(solution)/shard_map/rev | solution.py:75
  40.2 8.8 %all_gather.3 = bf16[4,3,8,8,128]{4,3,2,0,1:T(8,128)(2,1)S(1)} all-gather(bf16[1,3,8,8,128]{4,3,2,0,1:T(8,128)(2,1)S(1)} %pad_maximum_fusion.5), channel_id=1, replica_groups=mesh['gz'=8,'grp'=4] {'grp'}, dimensions={0}, use_global_device_ids=true | all-gather | bytes 245760 | tf_op jit(solution)/shard_map/all_gather | solution.py:123
  49.9 0.9 copy-done.22
  51.6 0.8 reshape.455
  52.4 1.5 multiply_convert_fusion.4
  53.9 0.9 copy.197
  54.7 0.9 fusion
  56.7 0.8 copy-done.41
  57.6 1.3 collective-permute-start.4
  58.9 1.3 collective-permute-start.5
  60.2 0.7 pad_maximum_fusion
  61.0 3.4 %collective-permute-done.5 = bf16[4,1,8,8,32]{4,3,2,0,1:T(8,128)(2,1)S(1)} collective-permute-done((bf16[4,1,8,8,32]{4,3,2,0,1:T(8,128)(2,1)S(1)}, bf16[4,1,8,8,32]{4,3,2,0,1:T(8,128)(2,1)S(1)}, u32[]{:S(2)}, u32[]{:S(2)}) %collective-permute-start.5) | collective-permute-done | bytes 16416 | tf_op jit(solution)/shard_map/ppermute | solution.py:15
  66.9 0.7 copy-done.58
  67.7 0.8 copy-done.46
  70.8 0.8 fusion.4
  74.9 43.0 %all-reduce.9.cloned.1.call-done = bf16[3456,32]{0,1:T(8,128)(2,1)} async-done(((bf16[3456,32]{0,1:T(8,128)(2,1)}), bf16[3456,32]{0,1:T(8,128)(2,1)}) %all-reduce.9.cloned.1.call-update) | async-done | bytes 221200 | tf_op jit(solution)/shard_map/psum | solution.py:106
  117.8 1.7 convert_element_type.157
  119.6 1.0 multiply_convert_fusion
  121.5 1.9 collective-permute-start.6
  123.4 1.5 collective-permute-start.7
  124.9 0.9 fusion.37
  126.2 0.9 concatenate.174
  127.2 2.1 collective-permute-done.7
  129.9 1.1 fusion.42
  131.3 1.6 copy.184
  132.9 1.6 copy.185
  134.5 1.6 copy.186
  136.1 1.6 copy.187
  138.0 0.7 copy-done.50
  138.8 0.8 copy-done.51
  139.6 0.9 copy-done.19
  140.6 0.8 copy-done.48
  141.4 0.9 copy-done.27
  145.8 0.8 convert_element_type.151
  146.6 113.2 %all-reduce.11.cloned.1.call-done = (f32[1728,64]{0,1:T(8,128)}, f32[512,128]{1,0:T(8,128)}) async-done(((f32[1728,64]{0,1:T(8,128)}, f32[512,128]{1,0:T(8,128)}), (f32[1728,64]{0,1:T(8,128)}, f32[512,128]{1,0:T(8,128)})) %all-reduce.11.cloned.1.call-update) | async-done | bytes 704528 | tf_op jit(solution)/shard_map/psum | solution.py:149
  259.8 1.9 copy.254
  261.7 0.7 copy.255
  (234 shorter events, 26.3 us)
Async XLA Ops:
  8.0 18.0 %copy-start = (bf16[512,128]{1,0:T(8,128)(2,1)S(1)}, bf16[512,128]{1,0:T(8,128)(2,1)}, u32[]{:S(2)}) copy-start(bf16[512,128]{1,0:T(8,128)(2,1)} %param.8) | copy-start | bytes 393220
  8.0 109.8 %all-reduce.9.cloned.1.call-start = ((), (), s32[]{:S(2)}) async-start(), calls=%async_computation.1 | async-start | bytes 442368 | tf_op jit(solution)/shard_map/psum | solution.py:106
  8.1 5.0 %copy-start.47 = (bf16[1,2,16,1024]{3,2,1,0:T(8,128)(2,1)S(1)}, bf16[1,2,16,1024]{3,2,1,0:T(8,128)(2,1)}, u32[]{:S(2)}) copy-start(bf16[1,2,16,1024]{3,2,1,0:T(8,128)(2,1)} %param.5) | copy-start | bytes 196612
  9.1 4.0 %copy-start.21 = (bf16[3456,32]{0,1:T(8,128)(2,1)S(1)}, bf16[3456,32]{0,1:T(8,128)(2,1)}, u32[]{:S(2)}) copy-start(bf16[3456,32]{0,1:T(8,128)(2,1)} %param.9) | copy-start | bytes 663556
  9.2 4.8 %collective-permute-start = (bf16[1,1,16,16,64]{4,3,2,1,0:T(8,128)(2,1)S(1)}, bf16[1,1,16,16,64]{4,3,2,1,0:T(8,128)(2,1)S(1)}, u32[]{:S(2)}, u32[]{:S(2)}) collective-permute-start(bf16[1,1,16,16,64]{4,3,2,1,0:T(8,128)(2,1)S(1)} %get-tuple-element.108), channel_id=1, source_target_pairs={{0,4},{4,8},{8,12},{12,16},{16,20},{20,24},{24,28},{1,5},{5,9},{9,... | collective-permute-start | bytes 98312 | tf_op jit(solution)/shard_map/ppermute | solution.py:14
  11.7 5.3 %collective-permute-start.1 = (bf16[1,1,16,16,64]{4,3,2,1,0:T(8,128)(2,1)S(1)}, bf16[1,1,16,16,64]{4,3,2,1,0:T(8,128)(2,1)S(1)}, u32[]{:S(2)}, u32[]{:S(2)}) collective-permute-start(bf16[1,1,16,16,64]{4,3,2,1,0:T(8,128)(2,1)S(1)} %get-tuple-element.109), channel_id=1, source_target_pairs={{4,0},{8,4},{12,8},{16,12},{20,16},{24,20},{28,24},{5,1},{9,5},{13... | collective-permute-start | bytes 98312 | tf_op jit(solution)/shard_map/ppermute | solution.py:15
  18.5 0.9 copy-start.16
  18.5 1.2 copy-start.20
  20.7 0.9 copy-start.36
  20.7 1.0 copy-start.37
  20.7 1.0 copy-start.38
  21.7 1.9 copy-start.35
  22.2 1.4 copy-start.28
  22.2 1.4 copy-start.29
  22.2 1.4 copy-start.30
  22.2 1.4 copy-start.31
  22.3 1.4 copy-start.32
  22.3 1.4 copy-start.33
  22.3 1.4 copy-start.34
  26.6 13.5 %collective-permute-start.2 = (bf16[1,1,8,8,128]{4,3,2,0,1:T(8,128)(2,1)S(1)}, bf16[1,1,8,8,128]{4,3,2,0,1:T(8,128)(2,1)S(1)}, u32[]{:S(2)}, u32[]{:S(2)}) collective-permute-start(bf16[1,1,8,8,128]{4,3,2,0,1:T(8,128)(2,1)S(1)} %fusion.6), channel_id=1, source_target_pairs={{0,4},{4,8},{8,12},{12,16},{16,20},{20,24},{24,28},{1,5},{5,9},{9,... | collective-permute-start | bytes 49160 | tf_op jit(solution)/shard_map/ppermute | solution.py:14
  31.5 8.7 %collective-permute-start.3 = (bf16[1,1,8,8,128]{4,3,2,0,1:T(8,128)(2,1)S(1)}, bf16[1,1,8,8,128]{4,3,2,0,1:T(8,128)(2,1)S(1)}, u32[]{:S(2)}, u32[]{:S(2)}) collective-permute-start(bf16[1,1,8,8,128]{4,3,2,0,1:T(8,128)(2,1)S(1)} %fusion.6), channel_id=1, source_target_pairs={{4,0},{8,4},{12,8},{16,12},{20,16},{24,20},{28,24},{5,1},{9,5},{13... | collective-permute-start | bytes 49160 | tf_op jit(solution)/shard_map/ppermute | solution.py:15
  49.8 0.9 copy-start.22
  56.6 0.9 copy-start.41
  57.5 2.7 copy-start.44
  57.6 3.4 %collective-permute-start.4 = (bf16[4,1,8,8,32]{4,3,2,0,1:T(8,128)(2,1)S(1)}, bf16[4,1,8,8,32]{4,3,2,0,1:T(8,128)(2,1)S(1)}, u32[]{:S(2)}, u32[]{:S(2)}) collective-permute-start(bf16[4,1,8,8,32]{4,3,2,0,1:T(8,128)(2,1)S(1)} %fusion.23), channel_id=1, source_target_pairs={{0,4},{4,8},{8,12},{12,16},{16,20},{20,24},{24,28},{1,5},{5,9},{9,... | collective-permute-start | bytes 49160 | tf_op jit(solution)/shard_map/ppermute | solution.py:14
  58.9 5.5 %collective-permute-start.5 = (bf16[4,1,8,8,32]{4,3,2,0,1:T(8,128)(2,1)S(1)}, bf16[4,1,8,8,32]{4,3,2,0,1:T(8,128)(2,1)S(1)}, u32[]{:S(2)}, u32[]{:S(2)}) collective-permute-start(bf16[4,1,8,8,32]{4,3,2,0,1:T(8,128)(2,1)S(1)} %fusion.23), channel_id=1, source_target_pairs={{4,0},{8,4},{12,8},{16,12},{20,16},{24,20},{28,24},{5,1},{9,5},{13... | collective-permute-start | bytes 49160 | tf_op jit(solution)/shard_map/ppermute | solution.py:15
  60.9 58.6 %reduce-scatter.4.cloned.1.call-start = ((), (), s32[]{:S(2)}) async-start(), calls=%async_computation.2 | async-start | bytes 81920
  65.9 0.9 copy-start.57
  69.9 1.8 copy-start.3
  71.6 188.2 %all-reduce.11.cloned.1.call-start = ((), (), s32[]{:S(2)}) async-start(), calls=%async_computation.3 | async-start | bytes 1441792 | tf_op jit(solution)/shard_map/psum | solution.py:149
  71.9 2.1 copy-start.15
  71.9 2.1 copy-start.17
  72.6 1.4 copy-start.9
  72.6 1.4 copy-start.11
  72.6 1.4 copy-start.13
  73.3 1.0 copy-start.5
  73.3 1.1 copy-start.7
  74.9 44.7 %copy-start.2 = (f32[512,64]{1,0:T(8,128)S(1)}, f32[512,64]{1,0:T(8,128)}, u32[]{:S(2)}) copy-start(f32[512,64]{1,0:T(8,128)} %copy-done.1) | copy-start | bytes 393220
  121.4 3.5 %copy-start.24 = (bf16[64,512]{1,0:T(8,128)(2,1)S(1)}, bf16[64,512]{1,0:T(8,128)(2,1)}, u32[]{:S(2)}) copy-start(bf16[64,512]{1,0:T(8,128)(2,1)} %copy-done.23) | copy-start | bytes 196612
  121.4 3.5 %copy-start.59 = (bf16[1,1,8,8,128]{4,3,2,1,0:T(8,128)(2,1)S(1)}, bf16[1,1,8,8,128]{4,3,2,1,0:T(8,128)(2,1)}, u32[]{:S(2)}) copy-start(bf16[1,1,8,8,128]{4,3,2,1,0:T(8,128)(2,1)} %reduce-scatter.4.cloned.1.call-done) | copy-start | bytes 49156
  121.5 5.7 %collective-permute-start.6 = (bf16[1,1,16,16,64]{4,3,2,1,0:T(8,128)(2,1)S(1)}, bf16[1,1,16,16,64]{4,3,2,1,0:T(8,128)(2,1)S(1)}, u32[]{:S(2)}, u32[]{:S(2)}) collective-permute-start(bf16[1,1,16,16,64]{4,3,2,1,0:T(8,128)(2,1)S(1)} %get-tuple-element.104), channel_id=1, source_target_pairs={{0,4},{4,8},{8,12},{12,16},{16,20},{20,24},{24,28},{1,5},{5,9},{9,... | collective-permute-start | bytes 98312 | tf_op jit(solution)/shard_map/ppermute | solution.py:14
  123.4 5.8 %collective-permute-start.7 = (bf16[1,1,16,16,64]{4,3,2,1,0:T(8,128)(2,1)S(1)}, bf16[1,1,16,16,64]{4,3,2,1,0:T(8,128)(2,1)S(1)}, u32[]{:S(2)}, u32[]{:S(2)}) collective-permute-start(bf16[1,1,16,16,64]{4,3,2,1,0:T(8,128)(2,1)S(1)} %get-tuple-element.105), channel_id=1, source_target_pairs={{4,0},{8,4},{12,8},{16,12},{20,16},{24,20},{28,24},{5,1},{9,5},{13... | collective-permute-start | bytes 98312 | tf_op jit(solution)/shard_map/ppermute | solution.py:15
  127.2 2.1 copy-start.53
  139.6 0.9 copy-start.19
  141.4 0.9 copy-start.27
  143.2 0.9 copy-start.26
  144.5 0.9 copy-start.25
  259.8 1.9 copy-start.52
  (23 other events, 18.0 us)
Sparse Core Ops, SparseCore 0:
  61.1 56.7 all-reduce.8
Sparse Core Ops, SparseCore 1:
  71.7 25.9 reduce-scatter.3
  127.2 132.5 all-reduce.10
where the time goes:
time: 271 us; the launch traced here: 270 us
  waiting for transfers between devices  165 us (61%)
  local copies, waits for them, and re-layouts  48.7 us (18%)
  between operations  16.6 us (6%)
  starting transfers between devices  16.1 us (6%)
  matrix products  9.78 us (4%)
  blocking collectives  8.84 us (3%)
  other arithmetic  4.97 us (2%)
    psum x1, waiting for transfers between devices, per_device(): fine_kg, down_kg = lax.psum((fine_kg, down_kg), ('gz', 'grp'))  113 us
    psum x1, waiting for transfers between devices, coarse_kernel_total(): lax.psum(partial_value.astype(jnp.bfloat16), 'gz').astype(jnp.float32)  43 us
    unnamed x156, local copies, waits for them, and re-layouts  19.7 us
    concatenate x30, local copies, waits for them, and re-layouts, convolve(): columns = jnp.concatenate(pieces, axis=-1).reshape(-1, 9 * channels)  11.2 us
    ppermute x4, starting transfers between devices, with_halo(): before = lax.ppermute(last, axis, up)  10.6 us
    all_gather x1, blocking collectives, per_device(): lax.all_gather(coarse_framed, 'grp', axis=0, tiled=True)  8.84 us
    ppermute x4, waiting for transfers between devices, with_halo(): after = lax.ppermute(initial, axis, down)  8.64 us
    dot_general x12, matrix products, convolve(): partial_value = jnp.dot(columns, rows, preferred_element_type=jnp.float32)  5.59 us
  transfers between devices with their start and end apart: 11, of which 5 were waited for; matrix products, arithmetic and copies ran while one was open for 11% of the time, Pallas kernels for 0%

commit v1 on v0

--- a/solution.py
+++ b/solution.py
@@ -2,6 +2,12 @@
 import jax.numpy as jnp
 from jax import lax
 from jax.sharding import PartitionSpec as P
+
+
+def add_all(shard, mesh_axis):
+    parts = lax.all_gather(shard, mesh_axis, axis=0, tiled=False)
+    acc = parts.sum(axis=0)
+    return acc
 
 
 def with_halo(array, sides, width):
@@ -103,7 +109,7 @@
 
 
 def coarse_kernel_total(partial_value):
-    return lax.psum(partial_value.astype(jnp.bfloat16), "gz").astype(jnp.float32)
+    return add_all(partial_value.astype(jnp.bfloat16), "gz").astype(jnp.float32)
 
 
 def per_device(volumes, cotangent, fine_kernel, down_kernel, coarse_kernel):

time: 271 us -> 252 us (0.930)
  waiting for transfers between devices: 165 us -> 135 us
  local copies, waits for them, and re-layouts: 48.7 us -> 54.5 us
  other arithmetic: 4.97 us -> 8.85 us
    psum x1 -> x0, waiting for transfers between devices: 43 us -> none  [coarse_kernel_total(): lax.psum(partial_value.astype(jnp.bfloat16), 'gz').astype(jnp.float32)]
    unnamed x4, waiting for transfers between devices: 0.05 us -> 19.6 us
    concatenate x30, local copies, waits for them, and re-layouts: 11.2 us -> 20.6 us  [convolve(): columns = jnp.concatenate(pieces, axis=-1).reshape(-1, 9 * channels)]
    unnamed x156 -> x128, local copies, waits for them, and re-layouts: 19.7 us -> 13.7 us
    psum x1, waiting for transfers between devices: 113 us -> 109 us  [per_device(): fine_kg, down_kg = lax.psum((fine_kg, down_kg), ('gz', 'grp'))]
  transfers between devices with their start and end apart: 11 -> 11, of which waited for: 5 -> 5; matrix products, arithmetic and copies ran while one was open for 11% -> 15% of each run, Pallas kernels for 0% -> 0%
where the time goes in v1:
time: 252 us; the launch traced here: 250 us
  waiting for transfers between devices  135 us (54%)
  local copies, waits for them, and re-layouts  54.5 us (22%)
  between operations  16.6 us (7%)
  starting transfers between devices  15.8 us (6%)
  matrix products  10.4 us (4%)
  other arithmetic  8.85 us (4%)
  blocking collectives  8.85 us (4%)
    psum x1, waiting for transfers between devices, per_device(): fine_kg, down_kg = lax.psum((fine_kg, down_kg), ('gz', 'grp'))  109 us
    concatenate x30, local copies, waits for them, and re-layouts, convolve(): columns = jnp.concatenate(pieces, axis=-1).reshape(-1, 9 * channels)  20.6 us
    unnamed x4, waiting for transfers between devices  19.6 us
    unnamed x128, local copies, waits for them, and re-layouts  13.7 us
    ppermute x4, starting transfers between devices, with_halo(): before = lax.ppermute(last, axis, up)  10.4 us
    all_gather x1, blocking collectives, per_device(): lax.all_gather(coarse_framed, 'grp', axis=0, tiled=True)  8.85 us
    dot_general x12, matrix products, convolve(): partial_value = jnp.dot(columns, rows, preferred_element_type=jnp.float32)  6.23 us
    ppermute x4, waiting for transfers between devices, with_halo(): after = lax.ppermute(initial, axis, down)  6.14 us
  transfers between devices with their start and end apart: 11, of which 5 were waited for; matrix products, arithmetic and copies ran while one was open for 15% of the time, Pallas kernels for 0%

profile of v1, /device:TPU:0, one launch (start us, length us, event | category | flops | bytes accessed | tf_op | source)
XLA Modules:
  0.0 250.1 jit_solution(6151217943517745373)
XLA Ops:
  8.1 1.0 reshape.491
  9.1 2.4 collective-permute-start
  11.5 1.3 collective-permute-start.1
  12.8 1.0 concatenate.148
  13.8 1.0 reshape.503
  15.5 1.3 collective-permute-done.1
  17.0 1.2 fusion.47
  19.5 1.0 fusion.29
  21.4 1.5 concatenate.143
  23.2 1.3 concatenate.155
  25.6 4.8 %collective-permute-start.2 = (bf16[1,1,8,8,128]{4,3,2,0,1:T(8,128)(2,1)S(1)}, bf16[1,1,8,8,128]{4,3,2,0,1:T(8,128)(2,1)S(1)}, u32[]{:S(2)}, u32[]{:S(2)}) collective-permute-start(bf16[1,1,8,8,128]{4,3,2,0,1:T(8,128)(2,1)S(1)} %fusion.9), channel_id=1, source_target_pairs={{0,4},{4,8},{8,12},{12,16},{16,20},{20,24},{24,28},{1,5},{5,9},{9,... | collective-permute-start | bytes 49160 | tf_op jit(solution)/shard_map/ppermute | solution.py:20
  30.4 1.3 collective-permute-start.3
  35.3 8.8 %all_gather.7 = bf16[4,3,8,8,128]{4,3,2,0,1:T(8,128)(2,1)S(1)} all-gather(bf16[1,3,8,8,128]{4,3,2,0,1:T(8,128)(2,1)S(1)} %pad_maximum_fusion.5), channel_id=1, replica_groups=mesh['gz'=8,'grp'=4] {'grp'}, dimensions={0}, use_global_device_ids=true | all-gather | bytes 245760 | tf_op jit(solution)/shard_map/all_gather | solution.py:129
  47.0 1.5 multiply_convert_fusion.4
  48.5 0.9 copy.197
  49.4 0.9 fusion.5
  50.5 0.9 copy.164
  51.4 1.0 fusion.26
  52.3 1.6 collective-permute-start.4
  54.0 1.3 collective-permute-start.5
  55.5 4.4 %collective-permute-done.5 = bf16[4,1,8,8,32]{4,3,2,0,1:T(8,128)(2,1)S(1)} collective-permute-done((bf16[4,1,8,8,32]{4,3,2,0,1:T(8,128)(2,1)S(1)}, bf16[4,1,8,8,32]{4,3,2,0,1:T(8,128)(2,1)S(1)}, u32[]{:S(2)}, u32[]{:S(2)}) %collective-permute-start.5) | collective-permute-done | bytes 16416 | tf_op jit(solution)/shard_map/ppermute | solution.py:21
  62.3 0.9 copy.167
  69.4 1.2 fusion.52
  70.6 1.1 concatenate.171
  72.0 1.1 concatenate.161
  75.1 1.7 rev.7
  79.2 1.2 concatenate.186
  80.4 19.5 %reduce-scatter.4.cloned.1.call-done = bf16[1,1,8,8,128]{4,3,2,1,0:T(8,128)(2,1)} async-done(((bf16[4,1,8,8,128]{4,3,2,1,0:T(8,128)(2,1)}), bf16[1,1,8,8,128]{4,3,2,1,0:T(8,128)(2,1)}) %reduce-scatter.4.cloned.1.call-update) | async-done | bytes 16400
  100.0 1.0 multiply_convert_fusion
  101.4 1.5 collective-permute-start.6
  102.9 1.5 collective-permute-start.7
  104.9 0.9 fusion.40
  106.2 0.9 concatenate.187
  108.6 1.2 fusion.45
  110.5 1.6 copy.184
  112.2 1.6 copy.185
  113.8 1.6 copy.186
  115.4 1.0 copy.187
  116.4 1.0 copy.188
  117.4 1.0 copy.189
  118.4 1.0 copy.190
  122.0 0.9 fusion.54
  123.0 1.0 pad_maximum_fusion.1
  123.9 1.2 concatenate.174
  127.3 1.8 reduce_sum.12
  129.9 109.3 %all-reduce.8.cloned.1.call-done = (f32[1728,64]{0,1:T(8,128)}, f32[512,128]{1,0:T(8,128)}) async-done(((f32[1728,64]{0,1:T(8,128)}, f32[512,128]{1,0:T(8,128)}), (f32[1728,64]{0,1:T(8,128)}, f32[512,128]{1,0:T(8,128)})) %all-reduce.8.cloned.1.call-update) | async-done | bytes 704528 | tf_op jit(solution)/shard_map/psum | solution.py:155
  239.2 1.8 copy.253
  241.0 1.7 copy.254
  (207 shorter events, 32.9 us)
Async XLA Ops:
  8.0 17.4 %copy-start = (bf16[512,128]{1,0:T(8,128)(2,1)S(1)}, bf16[512,128]{1,0:T(8,128)(2,1)}, u32[]{:S(2)}) copy-start(bf16[512,128]{1,0:T(8,128)(2,1)} %param.8) | copy-start | bytes 393220
  8.0 92.0 %reduce-scatter.4.cloned.1.call-start = ((), (), s32[]{:S(2)}) async-start(), calls=%async_computation.2 | async-start | bytes 81920
  9.1 6.4 %collective-permute-start = (bf16[1,1,16,16,64]{4,3,2,1,0:T(8,128)(2,1)S(1)}, bf16[1,1,16,16,64]{4,3,2,1,0:T(8,128)(2,1)S(1)}, u32[]{:S(2)}, u32[]{:S(2)}) collective-permute-start(bf16[1,1,16,16,64]{4,3,2,1,0:T(8,128)(2,1)S(1)} %get-tuple-element.108), channel_id=1, source_target_pairs={{0,4},{4,8},{8,12},{12,16},{16,20},{20,24},{24,28},{1,5},{5,9},{9,... | collective-permute-start | bytes 98312 | tf_op jit(solution)/shard_map/ppermute | solution.py:20
  11.5 5.3 %collective-permute-start.1 = (bf16[1,1,16,16,64]{4,3,2,1,0:T(8,128)(2,1)S(1)}, bf16[1,1,16,16,64]{4,3,2,1,0:T(8,128)(2,1)S(1)}, u32[]{:S(2)}, u32[]{:S(2)}) collective-permute-start(bf16[1,1,16,16,64]{4,3,2,1,0:T(8,128)(2,1)S(1)} %get-tuple-element.109), channel_id=1, source_target_pairs={{4,0},{8,4},{12,8},{16,12},{20,16},{24,20},{28,24},{5,1},{9,5},{13... | collective-permute-start | bytes 98312 | tf_op jit(solution)/shard_map/ppermute | solution.py:21
  18.2 3.0 %copy-start.3 = (bf16[1,2,16,16,64]{4,3,2,1,0:T(8,128)(2,1)}, bf16[1,2,16,16,64]{4,3,2,1,0:T(8,128)(2,1)S(1)}, u32[]{:S(2)}) copy-start(bf16[1,2,16,16,64]{4,3,2,1,0:T(8,128)(2,1)S(1)} %get-tuple-element.77) | copy-start | bytes 196612
  18.2 3.0 %copy-start.5 = (bf16[1,2,16,16,64]{4,3,2,1,0:T(8,128)(2,1)}, bf16[1,2,16,16,64]{4,3,2,1,0:T(8,128)(2,1)S(1)}, u32[]{:S(2)}) copy-start(bf16[1,2,16,16,64]{4,3,2,1,0:T(8,128)(2,1)S(1)} %get-tuple-element.78) | copy-start | bytes 196612
  18.3 3.0 %copy-start.7 = (bf16[1,2,16,16,64]{4,3,2,1,0:T(8,128)(2,1)}, bf16[1,2,16,16,64]{4,3,2,1,0:T(8,128)(2,1)S(1)}, u32[]{:S(2)}) copy-start(bf16[1,2,16,16,64]{4,3,2,1,0:T(8,128)(2,1)S(1)} %get-tuple-element.79) | copy-start | bytes 196612
  18.3 3.0 %copy-start.9 = (bf16[1,2,16,16,64]{4,3,2,1,0:T(8,128)(2,1)}, bf16[1,2,16,16,64]{4,3,2,1,0:T(8,128)(2,1)S(1)}, u32[]{:S(2)}) copy-start(bf16[1,2,16,16,64]{4,3,2,1,0:T(8,128)(2,1)S(1)} %get-tuple-element.80) | copy-start | bytes 196612
  18.3 3.0 %copy-start.11 = (bf16[1,2,16,16,64]{4,3,2,1,0:T(8,128)(2,1)}, bf16[1,2,16,16,64]{4,3,2,1,0:T(8,128)(2,1)S(1)}, u32[]{:S(2)}) copy-start(bf16[1,2,16,16,64]{4,3,2,1,0:T(8,128)(2,1)S(1)} %get-tuple-element.81) | copy-start | bytes 196612
  18.3 3.0 %copy-start.13 = (bf16[1,2,16,16,64]{4,3,2,1,0:T(8,128)(2,1)}, bf16[1,2,16,16,64]{4,3,2,1,0:T(8,128)(2,1)S(1)}, u32[]{:S(2)}) copy-start(bf16[1,2,16,16,64]{4,3,2,1,0:T(8,128)(2,1)S(1)} %get-tuple-element.82) | copy-start | bytes 196612
  18.3 6.3 %copy-start.15 = (bf16[1,2,16,16,64]{4,3,2,1,0:T(8,128)(2,1)}, bf16[1,2,16,16,64]{4,3,2,1,0:T(8,128)(2,1)S(1)}, u32[]{:S(2)}) copy-start(bf16[1,2,16,16,64]{4,3,2,1,0:T(8,128)(2,1)S(1)} %get-tuple-element.83) | copy-start | bytes 196612
  21.3 1.9 copy-start.26
  21.3 1.9 copy-start.27
  21.3 1.9 copy-start.28
  24.5 7.3 %copy-start.36 = (bf16[4,1,64,32]{2,3,1,0:T(8,128)(2,1)S(1)}, bf16[4,1,64,32]{2,3,1,0:T(8,128)(2,1)}, u32[]{:S(2)}) copy-start(bf16[4,1,64,32]{2,3,1,0:T(8,128)(2,1)} %param.6) | copy-start | bytes 49156
  24.9 10.4 %copy-start.16 = (f32[512,64]{0,1:T(8,128)}, f32[512,64]{0,1:T(8,128)S(1)}, u32[]{:S(2)}) copy-start(f32[512,64]{0,1:T(8,128)S(1)} %convolution_add_fusion.2) | copy-start | bytes 393220
  25.0 19.2 %copy-start.1 = (f32[512,64]{1,0:T(8,128)}, f32[512,64]{1,0:T(8,128)S(1)}, u32[]{:S(2)}) copy-start(f32[512,64]{1,0:T(8,128)S(1)} %copy.154) | copy-start | bytes 393220
  25.4 9.9 %copy-start.21 = (bf16[64,512]{1,0:T(8,128)(2,1)}, bf16[64,512]{1,0:T(8,128)(2,1)S(1)}, u32[]{:S(2)}) copy-start(bf16[64,512]{1,0:T(8,128)(2,1)S(1)} %reshape.495) | copy-start | bytes 196612
  25.6 9.7 %collective-permute-start.2 = (bf16[1,1,8,8,128]{4,3,2,0,1:T(8,128)(2,1)S(1)}, bf16[1,1,8,8,128]{4,3,2,0,1:T(8,128)(2,1)S(1)}, u32[]{:S(2)}, u32[]{:S(2)}) collective-permute-start(bf16[1,1,8,8,128]{4,3,2,0,1:T(8,128)(2,1)S(1)} %fusion.9), channel_id=1, source_target_pairs={{0,4},{4,8},{8,12},{12,16},{16,20},{20,24},{24,28},{1,5},{5,9},{9,... | collective-permute-start | bytes 49160 | tf_op jit(solution)/shard_map/ppermute | solution.py:20
  30.4 4.8 %collective-permute-start.3 = (bf16[1,1,8,8,128]{4,3,2,0,1:T(8,128)(2,1)S(1)}, bf16[1,1,8,8,128]{4,3,2,0,1:T(8,128)(2,1)S(1)}, u32[]{:S(2)}, u32[]{:S(2)}) collective-permute-start(bf16[1,1,8,8,128]{4,3,2,0,1:T(8,128)(2,1)S(1)} %fusion.9), channel_id=1, source_target_pairs={{4,0},{8,4},{12,8},{16,12},{20,16},{24,20},{28,24},{5,1},{9,5},{13... | collective-permute-start | bytes 49160 | tf_op jit(solution)/shard_map/ppermute | solution.py:21
  46.2 2.3 copy-start.31
  52.3 3.2 %collective-permute-start.4 = (bf16[4,1,8,8,32]{4,3,2,0,1:T(8,128)(2,1)S(1)}, bf16[4,1,8,8,32]{4,3,2,0,1:T(8,128)(2,1)S(1)}, u32[]{:S(2)}, u32[]{:S(2)}) collective-permute-start(bf16[4,1,8,8,32]{4,3,2,0,1:T(8,128)(2,1)S(1)} %fusion.26), channel_id=1, source_target_pairs={{0,4},{4,8},{8,12},{12,16},{16,20},{20,24},{24,28},{1,5},{5,9},{9,... | collective-permute-start | bytes 49160 | tf_op jit(solution)/shard_map/ppermute | solution.py:20
  54.0 6.0 %collective-permute-start.5 = (bf16[4,1,8,8,32]{4,3,2,0,1:T(8,128)(2,1)S(1)}, bf16[4,1,8,8,32]{4,3,2,0,1:T(8,128)(2,1)S(1)}, u32[]{:S(2)}, u32[]{:S(2)}) collective-permute-start(bf16[4,1,8,8,32]{4,3,2,0,1:T(8,128)(2,1)S(1)} %fusion.26), channel_id=1, source_target_pairs={{4,0},{8,4},{12,8},{16,12},{20,16},{24,20},{28,24},{5,1},{9,5},{13... | collective-permute-start | bytes 49160 | tf_op jit(solution)/shard_map/ppermute | solution.py:21
  55.5 4.4 %copy-start.40 = (bf16[4,1,8,8,32]{4,3,2,0,1:T(8,128)(2,1)}, bf16[4,1,8,8,32]{4,3,2,0,1:T(8,128)(2,1)S(1)}, u32[]{:S(2)}) copy-start(bf16[4,1,8,8,32]{4,3,2,0,1:T(8,128)(2,1)S(1)} %collective-permute-done.4) | copy-start | bytes 49156
  60.8 5.6 %copy-start.32 = (f32[256,32]{0,1:T(8,128)S(1)}, f32[256,32]{0,1:T(8,128)}, u32[]{:S(2)}) copy-start(f32[256,32]{0,1:T(8,128)} %copy-done.31) | copy-start | bytes 98308
  60.8 5.6 %copy-start.44 = (f32[256,32]{0,1:T(8,128)S(1)}, f32[256,32]{0,1:T(8,128)}, u32[]{:S(2)}) copy-start(f32[256,32]{0,1:T(8,128)} %reshape.520) | copy-start | bytes 98308
  60.8 8.6 %copy-start.39 = (bf16[1,3,3,32,128]{4,3,2,1,0:T(8,128)(2,1)S(1)}, bf16[1,3,3,32,128]{4,3,2,1,0:T(8,128)(2,1)}, u32[]{:S(2)}) copy-start(bf16[1,3,3,32,128]{4,3,2,1,0:T(8,128)(2,1)} %copy.175) | copy-start | bytes 221188
  61.6 10.1 %copy-start.38 = (bf16[1,3,3,32,128]{4,3,2,1,0:T(8,128)(2,1)S(1)}, bf16[1,3,3,32,128]{4,3,2,1,0:T(8,128)(2,1)}, u32[]{:S(2)}) copy-start(bf16[1,3,3,32,128]{4,3,2,1,0:T(8,128)(2,1)} %copy.176) | copy-start | bytes 221188
  62.3 10.7 %copy-start.35 = (bf16[1,3,3,32,128]{4,3,2,1,0:T(8,128)(2,1)S(1)}, bf16[1,3,3,32,128]{4,3,2,1,0:T(8,128)(2,1)}, u32[]{:S(2)}) copy-start(bf16[1,3,3,32,128]{4,3,2,1,0:T(8,128)(2,1)} %copy.165) | copy-start | bytes 221188
  64.3 9.6 %copy-start.37 = (bf16[1,1152,32]{1,2,0:T(8,128)(2,1)S(1)}, bf16[1,1152,32]{1,2,0:T(8,128)(2,1)}, u32[]{:S(2)}) copy-start(bf16[1,1152,32]{1,2,0:T(8,128)(2,1)} %fusion.5) | copy-start | bytes 221188
  69.4 5.3 %copy-start.19 = (bf16[1728,64]{0,1:T(8,128)(2,1)S(1)}, bf16[1728,64]{0,1:T(8,128)(2,1)}, u32[]{:S(2)}) copy-start(bf16[1728,64]{0,1:T(8,128)(2,1)} %param.7) | copy-start | bytes 663556
  73.9 53.4 %all-gather.2.cloned.1.call-start = ((), (), s32[]{:S(2)}) async-start(), calls=%async_computation.1 | async-start | bytes 1990656 | tf_op jit(solution)/shard_map/all_gather | solution.py:8
  74.7 164.5 %all-reduce.8.cloned.1.call-start = ((), (), s32[]{:S(2)}) async-start(), calls=%async_computation.3 | async-start | bytes 1441792 | tf_op jit(solution)/shard_map/psum | solution.py:155
  75.1 4.1 %copy-start.4 = (bf16[1,2,16,16,64]{4,3,2,1,0:T(8,128)(2,1)S(1)}, bf16[1,2,16,16,64]{4,3,2,1,0:T(8,128)(2,1)}, u32[]{:S(2)}) copy-start(bf16[1,2,16,16,64]{4,3,2,1,0:T(8,128)(2,1)} %copy-done.3) | copy-start | bytes 196612
  75.1 4.1 %copy-start.6 = (bf16[1,2,16,16,64]{4,3,2,1,0:T(8,128)(2,1)S(1)}, bf16[1,2,16,16,64]{4,3,2,1,0:T(8,128)(2,1)}, u32[]{:S(2)}) copy-start(bf16[1,2,16,16,64]{4,3,2,1,0:T(8,128)(2,1)} %copy-done.5) | copy-start | bytes 196612
  75.1 4.1 %copy-start.8 = (bf16[1,2,16,16,64]{4,3,2,1,0:T(8,128)(2,1)S(1)}, bf16[1,2,16,16,64]{4,3,2,1,0:T(8,128)(2,1)}, u32[]{:S(2)}) copy-start(bf16[1,2,16,16,64]{4,3,2,1,0:T(8,128)(2,1)} %copy-done.7) | copy-start | bytes 196612
  75.1 4.1 %copy-start.10 = (bf16[1,2,16,16,64]{4,3,2,1,0:T(8,128)(2,1)S(1)}, bf16[1,2,16,16,64]{4,3,2,1,0:T(8,128)(2,1)}, u32[]{:S(2)}) copy-start(bf16[1,2,16,16,64]{4,3,2,1,0:T(8,128)(2,1)} %copy-done.9) | copy-start | bytes 196612
  76.9 2.3 copy-start.12
  76.9 2.3 copy-start.14
  76.9 23.1 %copy-start.2 = (f32[512,64]{1,0:T(8,128)S(1)}, f32[512,64]{1,0:T(8,128)}, u32[]{:S(2)}) copy-start(f32[512,64]{1,0:T(8,128)} %copy-done.1) | copy-start | bytes 393220
  100.9 4.0 %copy-start.22 = (bf16[64,512]{1,0:T(8,128)(2,1)S(1)}, bf16[64,512]{1,0:T(8,128)(2,1)}, u32[]{:S(2)}) copy-start(bf16[64,512]{1,0:T(8,128)(2,1)} %copy-done.21) | copy-start | bytes 196612
  101.0 4.0 %copy-start.45 = (bf16[1,1,8,8,128]{4,3,2,1,0:T(8,128)(2,1)S(1)}, bf16[1,1,8,8,128]{4,3,2,1,0:T(8,128)(2,1)}, u32[]{:S(2)}) copy-start(bf16[1,1,8,8,128]{4,3,2,1,0:T(8,128)(2,1)} %reduce-scatter.4.cloned.1.call-done) | copy-start | bytes 49156
  101.4 5.8 %collective-permute-start.6 = (bf16[1,1,16,16,64]{4,3,2,1,0:T(8,128)(2,1)S(1)}, bf16[1,1,16,16,64]{4,3,2,1,0:T(8,128)(2,1)S(1)}, u32[]{:S(2)}, u32[]{:S(2)}) collective-permute-start(bf16[1,1,16,16,64]{4,3,2,1,0:T(8,128)(2,1)S(1)} %get-tuple-element.104), channel_id=1, source_target_pairs={{0,4},{4,8},{8,12},{12,16},{16,20},{20,24},{24,28},{1,5},{5,9},{9,... | collective-permute-start | bytes 98312 | tf_op jit(solution)/shard_map/ppermute | solution.py:20
  102.9 4.7 %collective-permute-start.7 = (bf16[1,1,16,16,64]{4,3,2,1,0:T(8,128)(2,1)S(1)}, bf16[1,1,16,16,64]{4,3,2,1,0:T(8,128)(2,1)S(1)}, u32[]{:S(2)}, u32[]{:S(2)}) collective-permute-start(bf16[1,1,16,16,64]{4,3,2,1,0:T(8,128)(2,1)S(1)} %get-tuple-element.105), channel_id=1, source_target_pairs={{4,0},{8,4},{12,8},{16,12},{20,16},{24,20},{28,24},{5,1},{9,5},{13... | collective-permute-start | bytes 98312 | tf_op jit(solution)/shard_map/ppermute | solution.py:21
  109.7 12.2 %copy-start.17 = (f32[512,64]{0,1:T(8,128)S(1)}, f32[512,64]{0,1:T(8,128)}, u32[]{:S(2)}) copy-start(f32[512,64]{0,1:T(8,128)} %copy-done.16) | copy-start | bytes 393220
  110.4 11.6 %copy-start.25 = (bf16[1,3,3,64,64]{4,3,2,1,0:T(8,128)(2,1)S(1)}, bf16[1,3,3,64,64]{4,3,2,1,0:T(8,128)(2,1)}, u32[]{:S(2)}) copy-start(bf16[1,3,3,64,64]{4,3,2,1,0:T(8,128)(2,1)} %copy.191) | copy-start | bytes 221188
  122.0 3.2 %copy-start.24 = (bf16[1,3,3,64,64]{4,3,2,1,0:T(8,128)(2,1)S(1)}, bf16[1,3,3,64,64]{4,3,2,1,0:T(8,128)(2,1)}, u32[]{:S(2)}) copy-start(bf16[1,3,3,64,64]{4,3,2,1,0:T(8,128)(2,1)} %copy.180) | copy-start | bytes 221188
  123.0 2.2 copy-start.34
  (9 other events, 10.2 us)
Sparse Core Ops, SparseCore 0:
  74.0 25.9 reduce-scatter.3
  107.3 131.8 all-reduce.7
Sparse Core Ops, SparseCore 1:
  76.6 28.2 all-gather.1
